TPU v7x, 32 devices: a whole 2x2x4 slice. The times are simulated.
32 devices in a mesh: groups: 2 (over y), space: 8 (over z, x), section: 2 (over core).
Axes of the slice: x: 2, y: 2, z: 4, core: 2. Of those that a mesh axis runs over, the one named last changes fastest.
Arguments:
- atm_state: bfloat16 [4, 8, 256, 256], P(('groups', 'section'), 'space'), parts along dimension 0, may hold values from -6 to 6
- ocean_state: bfloat16 [4, 2048, 192], P(('groups', 'section'), 'space'), parts along dimension 0, may hold values from -6 to 6
- owners: int32 [8, 256, 2], P('space'), may hold values from 0 to 7, all different within a row; in each aligned block of 256 rows (0 to 255, 256 to 511, ..., all dimensions but the last counted through in order) at most 128 rows name the same one
- target_cell: int32 [8, 256, 2], P('space'), may hold values from 0 to 255
- margin_weight: float32 [8, 256, 2], P('space'), may hold values from 0.25 to 1
- sea_mask: int32 [8, 256], P('space'), may hold values 0 or 1
- conv_kernel: bfloat16 [9, 256, 256], replicated, may hold values from -0.125 to 0.125
- meridional_weight: bfloat16 [256, 256], replicated, may hold values from -0.375 to 0.375
- atm_gain: float32 [256], replicated, may hold values from 0.25 to 1.75
- atm_in: bfloat16 [256, 1024], replicated, may hold values from -0.375 to 0.375
- atm_out: bfloat16 [1024, 256], replicated, may hold values from -0.1875 to 0.1875
- flux_weight: bfloat16 [256, 128], replicated, may hold values from -0.375 to 0.375
- forcing_weight: bfloat16 [128, 192], replicated, may hold values from -0.5 to 0.5
- ocean_gain: float32 [192], replicated, may hold values from 0.25 to 1.75
- ocean_in: bfloat16 [192, 768], replicated, may hold values from -0.4375 to 0.4375
- ocean_out: bfloat16 [768, 192], replicated, may hold values from -0.21875 to 0.21875
- surface_weight: bfloat16 [192, 128], replicated, may hold values from -0.4375 to 0.4375
- feedback_weight: bfloat16 [128, 256], replicated, may hold values from -0.5 to 0.5
Outputs:
- atm_next: bfloat16 [4, 8, 256, 256], P(('groups', 'section'), 'space'), parts along dimension 0
- ocean_next: bfloat16 [4, 2048, 192], P(('groups', 'section'), 'space'), parts along dimension 0
There are 2 independent parts, one for each index of `groups`. A program takes and returns all parts, laid end to end along the dimension named above; an argument that names none is the same for every part. Nothing has to cross between parts.
Inputs may be any that keep to these rules, and one draw needn't show every extreme that they name: Within the 256 cells of one latitude band, no owner is named by more than 128 margin entries, a bound that some block reaches; the 2 owners of one cell differ.
All inputs are finite; a program needn't handle non-finite values. No bound on the sum of `sea_mask` on one device may be relied on, other than what follows from the above.
Results may differ from a plain program's by a relative error of at most 0.014.
Values may be sent and summed in bfloat16 or wider, within the bound.
A program may use at most 64 MiB of HBM per device.

v0:
```python
import math
import jax
import jax.numpy as jnp
from jax import lax
from jax.sharding import PartitionSpec as P


def extended(cells, sides, width):
    for axis, dim in sides:
        count = lax.axis_size(axis)
        ends = count - 1
        head = lax.slice_in_dim(cells, 0, width, axis=dim)
        tail = lax.slice_in_dim(cells, cells.shape[dim] - width, cells.shape[dim], axis=dim)
        cells = jnp.concatenate(
            [
                lax.ppermute(tail, axis, [(i, (i + 1) % count) for i in range(ends)]),
                cells,
                lax.ppermute(head, axis, [((i + 1) % count, i) for i in range(ends)]),
            ],
            axis=dim,
        )
    return cells


def entering(part, axis, combine, identity):
    place = lax.axis_index(axis)
    gathered = lax.all_gather(part, axis)
    state = jnp.zeros_like(part) + jnp.asarray(identity, part.dtype)

    def one(hop, state):
        return combine(state, lax.dynamic_index_in_dim(gathered, hop, 0, False))

    return lax.fori_loop(0, place, one, state)


def conv_taps(padded, kernel, lat_rows):
    channels = padded.shape[-1]
    columns = []
    for row_off in range(3):
        lat_band = padded[row_off : row_off + lat_rows]
        for col_off in range(3):
            columns.append(jnp.roll(lat_band, 1 - col_off, axis=1))
    stacked = jnp.concatenate(columns, axis=-1)
    flattened = stacked.reshape(-1, 9 * channels)
    result = jnp.dot(
        flattened, kernel.reshape(9 * channels, channels), preferred_element_type=jnp.float32
    )
    return result.reshape(lat_rows, padded.shape[1], channels)


def rms_scale(values, gain_vec):
    return values * lax.rsqrt(jnp.mean(values * values, axis=-1, keepdims=True) + 1e-06) * gain_vec


def add_terms(earlier, later):
    return earlier + later


def contract_first(left, right):
    return lax.dot_general(
        left, right, (((0,), (0,)), ((), ())), preferred_element_type=jnp.float32
    )


def local(
    atm_state,
    ocean_state,
    owners,
    target_cell,
    margin_weight,
    sea_mask,
    conv_kernel,
    meridional_weight,
    atm_gain,
    atm_in,
    atm_out,
    flux_weight,
    forcing_weight,
    ocean_gain,
    ocean_in,
    ocean_out,
    surface_weight,
    feedback_weight,
):
    atm_one = atm_state[0]
    ocn_one = ocean_state[0]
    lat_rows, lon_cells, channels = atm_one.shape
    margin_count = owners.shape[-1]
    flux_width = flux_weight.shape[1]
    peer_count = lax.axis_size("space")
    slot_count = max(2, 2 * lat_rows * lon_cells * margin_count // peer_count)
    lat_total = lat_rows * peer_count
    padded = extended(atm_one, (("space", 0),), 1)
    mixing = conv_taps(padded, conv_kernel, lat_rows)
    hidden = atm_one.astype(jnp.float32) + mixing
    zonal_sums = jnp.sum(hidden, axis=1) / math.sqrt(lon_cells)
    band_total = jnp.sum(zonal_sums, axis=0)
    before = entering(band_total, "space", add_terms, jnp.zeros_like(band_total))
    prefix = (before[None, :] + jnp.cumsum(zonal_sums, axis=0) - zonal_sums) / math.sqrt(lat_total)
    meridional = jnp.dot(
        prefix, meridional_weight.astype(jnp.float32), precision=lax.Precision.HIGHEST
    )
    lifted = (hidden + meridional[:, None, :]).reshape(-1, channels)
    normed = rms_scale(lifted, atm_gain).astype(jnp.bfloat16)
    activated = jax.nn.silu(jnp.dot(normed, atm_in, preferred_element_type=jnp.float32)).astype(
        jnp.bfloat16
    )
    atm_mid = (lifted + jnp.dot(activated, atm_out, preferred_element_type=jnp.float32)).astype(
        jnp.bfloat16
    )
    flux_rows = jnp.dot(atm_mid, flux_weight, preferred_element_type=jnp.float32)
    sea_cells = sea_mask.astype(jnp.float32).reshape(-1)
    weights = margin_weight.reshape(-1, margin_count)
    payload = (weights[:, :, None] * sea_cells[:, None, None] * flux_rows[:, None, :]).astype(
        jnp.bfloat16
    )
    payload = payload.reshape(-1, flux_width)
    owner_ids = owners.reshape(-1)
    owner_hits = (owner_ids[:, None] == jnp.arange(peer_count, dtype=jnp.int32)[None, :]).astype(
        jnp.int32
    )
    slot_rank = jnp.sum((jnp.cumsum(owner_hits, axis=0) - 1) * owner_hits, axis=1)
    slot_index = owner_ids * slot_count + slot_rank
    slot_total = peer_count * slot_count
    placement = slot_index[:, None] == jnp.arange(slot_total, dtype=jnp.int32)[None, :]
    place_bf = placement.astype(jnp.bfloat16)
    send_rows = contract_first(place_bf, payload).astype(jnp.bfloat16)
    entry_cells = target_cell.reshape(-1)
    send_cells = jnp.sum(placement.astype(jnp.int32) * entry_cells[:, None], axis=0)
    recv_rows, recv_cells = (
        lax.all_to_all(
            send_rows.reshape(peer_count, slot_count, flux_width),
            "space",
            split_axis=0,
            concat_axis=0,
            tiled=True,
        ),
        lax.all_to_all(
            send_cells.reshape(peer_count, slot_count),
            "space",
            split_axis=0,
            concat_axis=0,
            tiled=True,
        ),
    )
    recv_cells = recv_cells.reshape(-1)
    ocean_cells = ocn_one.shape[0]
    cell_onehot = (recv_cells[:, None] == jnp.arange(ocean_cells, dtype=jnp.int32)[None, :]).astype(
        jnp.bfloat16
    )
    forcing = contract_first(cell_onehot, recv_rows.reshape(-1, flux_width)).astype(jnp.bfloat16)
    ocean_lift = ocn_one.astype(jnp.float32) + jnp.dot(
        forcing, forcing_weight, preferred_element_type=jnp.float32
    )
    ocean_normed = rms_scale(ocean_lift, ocean_gain).astype(jnp.bfloat16)
    ocean_act = jax.nn.silu(
        jnp.dot(ocean_normed, ocean_in, preferred_element_type=jnp.float32)
    ).astype(jnp.bfloat16)
    ocean_new = (
        ocean_lift + jnp.dot(ocean_act, ocean_out, preferred_element_type=jnp.float32)
    ).astype(jnp.bfloat16)
    surface = jnp.dot(ocean_new, surface_weight, preferred_element_type=jnp.float32).astype(
        jnp.bfloat16
    )
    back_rows = jnp.dot(cell_onehot, surface, preferred_element_type=jnp.float32).astype(
        jnp.bfloat16
    )
    returned = lax.all_to_all(
        back_rows.reshape(peer_count, slot_count, flux_width),
        "space",
        split_axis=0,
        concat_axis=0,
        tiled=True,
    )
    picked = jnp.dot(place_bf, returned.reshape(-1, flux_width), preferred_element_type=jnp.float32)
    picked = picked.reshape(-1, margin_count, flux_width)
    feedback = jnp.sum(weights[:, :, None] * picked, axis=1).astype(jnp.bfloat16)
    back_term = jnp.dot(feedback, feedback_weight, preferred_element_type=jnp.float32)
    atm_new = (atm_mid.astype(jnp.float32) + sea_cells[:, None] * back_term).astype(jnp.bfloat16)
    return (atm_new.reshape(1, lat_rows, lon_cells, channels), ocean_new[None])


def solution(mesh):
    placed = (
        P(("groups", "section"), "space", None, None),
        P(("groups", "section"), "space", None),
        P("space", None, None),
        P("space", None, None),
        P("space", None, None),
        P("space", None),
        P(),
        P(),
        P(),
        P(),
        P(),
        P(),
        P(),
        P(),
        P(),
        P(),
        P(),
        P(),
    )
    return jax.shard_map(
        local,
        mesh=mesh,
        in_specs=placed,
        out_specs=(
            P(("groups", "section"), "space", None, None),
            P(("groups", "section"), "space", None),
        ),
        check_vma=False,
    )
```

profile of v0, /device:TPU:0, one launch (start us, length us, event | category | flops | bytes accessed | tf_op | source)
XLA Modules:
  0.0 71.0 jit_solution(671286517310417763)
XLA Ops:
  0.7 5.0 %collective-permute-start = (bf16[1,256,256]{2,1,0:T(8,128)(2,1)}, bf16[1,256,256]{2,1,0:T(8,128)(2,1)S(1)}, u32[]{:S(2)}, u32[]{:S(2)}) collective-permute-start(bf16[1,256,256]{2,1,0:T(8,128)(2,1)} %bitcast.71), channel_id=1, source_target_pairs={{0,2},{2,4},{4,6},{6,8},{8,10},{10,12},{12,14},{1,3},{3,5},{5,7},{... | collective-permute-start | bytes 393224 | tf_op jit(solution)/shard_map/ppermute | solution.py:16
  5.7 1.3 %collective-permute-start.1 = (bf16[1,256,256]{2,1,0:T(8,128)(2,1)}, bf16[1,256,256]{2,1,0:T(8,128)(2,1)S(1)}, u32[]{:S(2)}, u32[]{:S(2)}) collective-permute-start(bf16[1,256,256]{2,1,0:T(8,128)(2,1)} %bitcast.72), channel_id=1, source_target_pairs={{2,0},{4,2},{6,4},{8,6},{10,8},{12,10},{14,12},{3,1},{5,3},{7,5},{... | collective-permute-start | bytes 393224 | tf_op jit(solution)/shard_map/ppermute | solution.py:18
  7.0 0.8 %copy.35 = s32[1,256,2]{2,1,0:T(8,128)S(1)} copy(s32[1,256,2]{1,2,0:T(2,128)} %param.22) | data formatting | bytes 4096 | tf_op args[2]
  8.1 1.1 %reduce-window.6 = s32[8,4,128]{2,0,1:T(8,128)S(1)} reduce-window(s32[8,4,128]{2,0,1:T(8,128)S(1)} %fusion.41, s32[]{:T(128)} %constant.39.clone.1), window={size=1x1x128 pad=0_0x0_0x127_0}, to_apply=%region_4.5 | reduce-window | flops 520192 | bytes 32772 | tf_op jit(solution)/shard_map/reduce-window
  9.3 0.2 slice_reduce_fusion
  9.6 0.8 %copy.39 = s32[1,256,2]{2,1,0:T(8,128)S(1)} copy(s32[1,256,2]{1,2,0:T(2,128)} %param.23) | data formatting | bytes 4096 | tf_op args[3]
  10.6 0.9 %select_reduce_fusion = s32[1024]{0:T(1024)} fusion(s32[512]{0:T(512)S(1)} %mul.144, s32[512]{0:T(512)S(1)} %multiply_add_fusion), kind=kLoop, calls=%fused_computation.1 | loop fusion | flops 1571840 | bytes 8192 | tf_op jit(solution)/shard_map/reduce_sum | solution.py:129
  11.5 7.0 %all-to-all-start = ((s32[8,1,128]{2,1,0:T(1,128)}), s32[8,1,128]{2,1,0:T(1,128)S(1)}, u32[]{:S(2)}, u32[]{:S(2)}) async-start(s32[8,1,128]{2,1,0:T(1,128)} %bitcast.14), calls=%async_computation | async-start | bytes 8192 | tf_op jit(solution)/shard_map/all_to_all | solution.py:138
  18.4 1.0 %fusion.47 = (bf16[1,255,256]{2,1,0:T(8,128)(2,1)S(1)}, bf16[1,255,256]{2,1,0:T(8,128)(2,1)S(1)}) fusion(bf16[1,256,256]{2,1,0:T(8,128)(2,1)} %bitcast.73), kind=kLoop, calls=%fused_computation.73 | loop fusion | bytes 522240 | tf_op jit(solution)/shard_map/jit(_roll_static)/slice | solution.py:42
  20.5 0.5 fusion.51
  21.0 21.0 %all-gather.1 = f32[8,1,256]{2,1,0:T(1,128)S(1)} all-gather(f32[1,1,256]{2,1,0:T(1,128)S(1)} %bitcast.86), channel_id=2, replica_groups=mesh['groups'=2,'space'=8,'section'=2] {'space'}, dimensions={0}, use_global_device_ids=true | all-gather | bytes 9216 | tf_op jit(solution)/shard_map/all_gather | solution.py:27
  42.2 0.2 multiply_reduce_fusion
  42.4 0.6 fusion.18
  43.0 0.2 copy-done.3
  43.2 0.2 fusion.53
  43.5 0.9 %fusion.4 = bf16[1024,128]{1,0:T(8,128)(2,1)S(1)} fusion(s32[512]{0:T(512)S(1)} %multiply_add_fusion, f32[512,128]{1,0:T(8,128)S(1)} %bitcast.75, f32[512]{0:T(512)S(1)} %mul.149), kind=kOutput, calls=%fused_computation.7 | convolution fusion | flops 135004160 | bytes 528384 | tf_op jit(solution)/shard_map/dot_general | solution.py:60
  44.4 10.6 %all_to_all.19 = bf16[8,128,128]{2,1,0:T(8,128)(2,1)S(1)} all-to-all(bf16[8,128,128]{2,1,0:T(8,128)(2,1)S(1)} %bitcast.77), channel_id=1, replica_groups=mesh['groups'=2,'space'=8,'section'=2] {'space'}, dimensions={0} | all-to-all | bytes 524288 | tf_op jit(solution)/shard_map/all_to_all | solution.py:131
  55.1 0.8 %multiply_reduce_fusion.1 = (f32[256]{0:T(256)S(1)}, f32[256,192]{0,1:T(8,128)S(1)}) fusion(bf16[128,192]{0,1:T(8,128)(2,1)S(1)} %copy-done.12, bf16[1024,128]{1,0:T(8,128)(2,1)S(1)} %bitcast.78, s32[1024]{0:T(1024)S(1)} %bitcast.87, bf16[1,256,192]{1,2,0:T(8,128)(2,1)S(1)} %copy-done.11), kind=kOutput, calls=%fused_computation.37 | convolution fusion | flops 80183040 | bytes 611328 | tf_op jit(solution)/shard_map/dot_general | solution.py:152
  55.9 0.7 fusion.19
  56.7 1.2 %convolution_convert_fusion = bf16[1024,128]{1,0:T(8,128)(2,1)} fusion(bf16[256,192]{0,1:T(8,128)(2,1)S(1)} %fusion.19, bf16[192,128]{1,0:T(8,128)(2,1)S(1)} %copy-done.13, s32[1024]{0:T(1024)S(1)} %bitcast.88), kind=kOutput, calls=%fused_computation.8 | convolution fusion | flops 80117760 | bytes 413696 | tf_op jit(solution)/shard_map/dot_general | solution.py:165
  58.0 3.5 %all-to-all-start.2 = ((bf16[8,128,128]{2,1,0:T(8,128)(2,1)}), bf16[8,128,128]{2,1,0:T(8,128)(2,1)S(1)}, u32[]{:S(2)}, u32[]{:S(2)}) async-start(bf16[8,128,128]{2,1,0:T(8,128)(2,1)} %bitcast.20), calls=%async_computation.2 | async-start | bytes 524288 | tf_op jit(solution)/shard_map/all_to_all | solution.py:168
  61.8 7.9 %all-to-all-done.2 = bf16[8,128,128]{2,1,0:T(8,128)(2,1)S(1)} async-done(((bf16[8,128,128]{2,1,0:T(8,128)(2,1)}), bf16[8,128,128]{2,1,0:T(8,128)(2,1)S(1)}, u32[]{:S(2)}, u32[]{:S(2)}) %all-to-all-start.2) | async-done | bytes 262176 | tf_op jit(solution)/shard_map/all_to_all | solution.py:168
  69.7 0.5 fusion.15
  70.2 0.8 %fusion.20 = bf16[1,1,256,256]{3,2,1,0:T(8,128)(2,1)} fusion(bf16[128,256]{1,0:T(8,128)(2,1)S(1)} %copy-done.4, bf16[256,256]{1,0:T(8,128)(2,1)S(1)} %fusion.18, f32[256]{0:T(256)S(1)} %bitcast.82, bf16[256,128]{1,0:T(8,128)(2,1)S(1)} %fusion.15), kind=kOutput, calls=%fused_computation.22 | convolution fusion | flops 17039360 | bytes 394240 | tf_op jit(solution)/shard_map/dot_general | solution.py:178
  (76 shorter events, 2.0 us)
Async XLA Ops:
  0.6 19.8 %copy-start = (bf16[9,256,256]{2,1,0:T(8,128)(2,1)S(1)}, bf16[9,256,256]{2,1,0:T(8,128)(2,1)}, u32[]{:S(2)}) copy-start(bf16[9,256,256]{2,1,0:T(8,128)(2,1)} %param.26) | copy-start | bytes 3538948
  0.6 19.4 %copy-start.1 = (bf16[1,1,256,256]{3,2,1,0:T(8,128)(2,1)S(1)}, bf16[1,1,256,256]{3,2,1,0:T(8,128)(2,1)}, u32[]{:S(2)}) copy-start(bf16[1,1,256,256]{3,2,1,0:T(8,128)(2,1)} %param.20) | copy-start | bytes 393220
  0.7 18.8 %copy-start.6 = (s32[1,256]{1,0:T(1,128)S(1)}, s32[1,256]{1,0:T(1,128)}, u32[]{:S(2)}) copy-start(s32[1,256]{1,0:T(1,128)} %param.25) | copy-start | bytes 3076
  0.7 19.1 %copy-start.5 = (f32[1,256,2]{1,2,0:T(2,128)S(1)}, f32[1,256,2]{1,2,0:T(2,128)}, u32[]{:S(2)}) copy-start(f32[1,256,2]{1,2,0:T(2,128)} %param.24) | copy-start | bytes 6148
  0.7 19.4 %collective-permute-start = (bf16[1,256,256]{2,1,0:T(8,128)(2,1)}, bf16[1,256,256]{2,1,0:T(8,128)(2,1)S(1)}, u32[]{:S(2)}, u32[]{:S(2)}) collective-permute-start(bf16[1,256,256]{2,1,0:T(8,128)(2,1)} %bitcast.71), channel_id=1, source_target_pairs={{0,2},{2,4},{4,6},{6,8},{8,10},{10,12},{12,14},{1,3},{3,5},{5,7},{... | collective-permute-start | bytes 393224 | tf_op jit(solution)/shard_map/ppermute | solution.py:16
  5.7 14.6 %collective-permute-start.1 = (bf16[1,256,256]{2,1,0:T(8,128)(2,1)}, bf16[1,256,256]{2,1,0:T(8,128)(2,1)S(1)}, u32[]{:S(2)}, u32[]{:S(2)}) collective-permute-start(bf16[1,256,256]{2,1,0:T(8,128)(2,1)} %bitcast.72), channel_id=1, source_target_pairs={{2,0},{4,2},{6,4},{8,6},{10,8},{12,10},{14,12},{3,1},{5,3},{7,5},{... | collective-permute-start | bytes 393224 | tf_op jit(solution)/shard_map/ppermute | solution.py:18
  11.5 32.9 %all-to-all-start = ((s32[8,1,128]{2,1,0:T(1,128)}), s32[8,1,128]{2,1,0:T(1,128)S(1)}, u32[]{:S(2)}, u32[]{:S(2)}) async-start(s32[8,1,128]{2,1,0:T(1,128)} %bitcast.14), calls=%async_computation | async-start | bytes 8192 | tf_op jit(solution)/shard_map/all_to_all | solution.py:138
  20.4 21.6 %copy-start.2 = (bf16[256,256]{1,0:T(8,128)(2,1)S(1)}, bf16[256,256]{1,0:T(8,128)(2,1)}, u32[]{:S(2)}) copy-start(bf16[256,256]{1,0:T(8,128)(2,1)} %param.27) | copy-start | bytes 393220
  20.5 21.9 %copy-start.7 = (bf16[1024,256]{1,0:T(8,128)(2,1)S(1)}, bf16[1024,256]{1,0:T(8,128)(2,1)}, u32[]{:S(2)}) copy-start(bf16[1024,256]{1,0:T(8,128)(2,1)} %param.30) | copy-start | bytes 1572868
  20.5 21.9 %copy-start.8 = (bf16[256,1024]{1,0:T(8,128)(2,1)S(1)}, bf16[256,1024]{1,0:T(8,128)(2,1)}, u32[]{:S(2)}) copy-start(bf16[256,1024]{1,0:T(8,128)(2,1)} %param.29) | copy-start | bytes 1572868
  20.5 21.9 %copy-start.14 = (f32[256]{0:T(256)S(1)}, f32[256]{0:T(256)}, u32[]{:S(2)}) copy-start(f32[256]{0:T(256)} %param.28) | copy-start | bytes 3076
  42.4 0.8 %copy-start.3 = (bf16[256,128]{1,0:T(8,128)(2,1)S(1)}, bf16[256,128]{1,0:T(8,128)(2,1)}, u32[]{:S(2)}) copy-start(bf16[256,128]{1,0:T(8,128)(2,1)} %param.31) | copy-start | bytes 196612
  43.2 11.9 %copy-start.11 = (bf16[1,256,192]{1,2,0:T(8,128)(2,1)S(1)}, bf16[1,256,192]{1,2,0:T(8,128)(2,1)}, u32[]{:S(2)}) copy-start(bf16[1,256,192]{1,2,0:T(8,128)(2,1)} %param.21) | copy-start | bytes 294916
  43.2 11.9 %copy-start.12 = (bf16[128,192]{0,1:T(8,128)(2,1)S(1)}, bf16[128,192]{0,1:T(8,128)(2,1)}, u32[]{:S(2)}) copy-start(bf16[128,192]{0,1:T(8,128)(2,1)} %param.32) | copy-start | bytes 147460
  43.5 12.4 %copy-start.9 = (bf16[768,192]{0,1:T(8,128)(2,1)S(1)}, bf16[768,192]{0,1:T(8,128)(2,1)}, u32[]{:S(2)}) copy-start(bf16[768,192]{0,1:T(8,128)(2,1)} %param.35) | copy-start | bytes 884740
  43.5 12.4 %copy-start.10 = (bf16[192,768]{1,0:T(8,128)(2,1)S(1)}, bf16[192,768]{1,0:T(8,128)(2,1)}, u32[]{:S(2)}) copy-start(bf16[192,768]{1,0:T(8,128)(2,1)} %param.34) | copy-start | bytes 884740
  43.5 12.4 %copy-start.15 = (f32[192]{0:T(256)S(1)}, f32[192]{0:T(256)}, u32[]{:S(2)}) copy-start(f32[192]{0:T(256)} %param.33) | copy-start | bytes 2308
  55.9 0.8 %copy-start.13 = (bf16[192,128]{1,0:T(8,128)(2,1)S(1)}, bf16[192,128]{1,0:T(8,128)(2,1)}, u32[]{:S(2)}) copy-start(bf16[192,128]{1,0:T(8,128)(2,1)} %param.36) | copy-start | bytes 147460
  56.7 13.5 %copy-start.16 = (bf16[256,192]{0,1:T(8,128)(2,1)}, bf16[256,192]{0,1:T(8,128)(2,1)S(1)}, u32[]{:S(2)}) copy-start(bf16[256,192]{0,1:T(8,128)(2,1)S(1)} %fusion.19) | copy-start | bytes 294916
  58.0 12.2 %copy-start.4 = (bf16[128,256]{1,0:T(8,128)(2,1)S(1)}, bf16[128,256]{1,0:T(8,128)(2,1)}, u32[]{:S(2)}) copy-start(bf16[128,256]{1,0:T(8,128)(2,1)} %param.37) | copy-start | bytes 196612
  58.0 11.7 %all-to-all-start.2 = ((bf16[8,128,128]{2,1,0:T(8,128)(2,1)}), bf16[8,128,128]{2,1,0:T(8,128)(2,1)S(1)}, u32[]{:S(2)}, u32[]{:S(2)}) async-start(bf16[8,128,128]{2,1,0:T(8,128)(2,1)} %bitcast.20), calls=%async_computation.2 | async-start | bytes 524288 | tf_op jit(solution)/shard_map/all_to_all | solution.py:168
where the time goes:
time: 71.6 us; the launch traced here: 71 us
  blocking collectives  31.6 us (44%)
  starting transfers between devices  16.8 us (23%)
  waiting for transfers between devices  7.92 us (11%)
  matrix products  6.33 us (9%)
  local copies, waits for them, and re-layouts  4.64 us (6%)
  other arithmetic  2.53 us (4%)
  between operations  1.17 us (2%)
    all_gather x1, blocking collectives, entering(): gathered = lax.all_gather(part, axis)  21 us
    all_to_all x1, blocking collectives, local(): lax.all_to_all(send_rows.reshape(peer_count, slot_count, flux_width), 'sp...  10.6 us
    all_to_all x1, waiting for transfers between devices, local(): lax.all_to_all(back_rows.reshape(peer_count, slot_count, flux_width), 'sp...  7.91 us
    all_to_all x1, starting transfers between devices, local(): lax.all_to_all(send_cells.reshape(peer_count, slot_count), 'space', split...  6.96 us
    ppermute x1, starting transfers between devices, extended(): lax.ppermute(tail, axis, [(i, (i + 1) % count) for i in range(ends)])  5.01 us
    all_to_all x1, starting transfers between devices, local(): lax.all_to_all(back_rows.reshape(peer_count, slot_count, flux_width), 'sp...  3.54 us
    unnamed x41, local copies, waits for them, and re-layouts  2.22 us
  transfers between devices with their start and end apart: 4, of which 1 were waited for; matrix products, arithmetic and copies ran while one was open for 13% of the time, Pallas kernels for 0%

commit v1 on v0

--- a/solution.py
+++ b/solution.py
@@ -3,6 +3,22 @@
 import jax.numpy as jnp
 from jax import lax
 from jax.sharding import PartitionSpec as P
+
+
+def exchange_in_pairs(x, axis, split, join):
+    ways, here = (lax.axis_size(axis), lax.axis_index(axis))
+    width = x.shape[split] // ways
+    shape = list(x.shape)
+    shape[split] = width
+    height = shape[join]
+    shape[join] = height * ways
+    full = jnp.zeros(shape, x.dtype)
+    for mask in range(ways):
+        part = lax.dynamic_slice_in_dim(x, (here ^ mask) * width, width, axis=split)
+        if mask:
+            part = lax.ppermute(part, axis, [(d, d ^ mask) for d in range(ways)])
+        full = lax.dynamic_update_slice_in_dim(full, part, (here ^ mask) * height, axis=join)
+    return full
 
 
 def extended(cells, sides, width):
@@ -135,13 +151,7 @@
             concat_axis=0,
             tiled=True,
         ),
-        lax.all_to_all(
-            send_cells.reshape(peer_count, slot_count),
-            "space",
-            split_axis=0,
-            concat_axis=0,
-            tiled=True,
-        ),
+        exchange_in_pairs(send_cells.reshape(peer_count, slot_count), "space", 0, 0),
     )
     recv_cells = recv_cells.reshape(-1)
     ocean_cells = ocn_one.shape[0]

time: 71.6 us -> 76.8 us (1.073)
  blocking collectives: 31.6 us -> 22 us
  starting transfers between devices: 16.8 us -> 24.5 us
  waiting for transfers between devices: 7.92 us -> 13.9 us
    ppermute x0 -> x7, starting transfers between devices: none -> 11.3 us  [exchange_in_pairs(): part = lax.ppermute(part, axis, [(d, d ^ mask) for d in range(ways)])]
    all_to_all x1 -> x0, blocking collectives: 10.6 us -> none  [local(): lax.all_to_all(send_rows.reshape(peer_count, slot_count, flux_width), 'sp...]
    ppermute x0 -> x7, waiting for transfers between devices: none -> 5.98 us  [exchange_in_pairs(): part = lax.ppermute(part, axis, [(d, d ^ mask) for d in range(ways)])]
    all_to_all x1, starting transfers between devices: 6.96 us -> 3.41 us  [local(): lax.all_to_all(send_rows.reshape(peer_count, slot_count, flux_width), 'sp...]
    all_gather x1, blocking collectives: 21 us -> 22 us  [entering(): gathered = lax.all_gather(part, axis)]
  transfers between devices with their start and end apart: 4 -> 11, of which waited for: 1 -> 4; matrix products, arithmetic and copies ran while one was open for 13% -> 9% of each run, Pallas kernels for 0% -> 0%
where the time goes in v1:
time: 76.8 us; the launch traced here: 76.2 us
  starting transfers between devices  24.5 us (32%)
  blocking collectives  22 us (29%)
  waiting for transfers between devices  13.9 us (18%)
  matrix products  7.04 us (9%)
  local copies, waits for them, and re-layouts  4.93 us (6%)
  other arithmetic  2.61 us (3%)
  between operations  1.27 us (2%)
    all_gather x1, blocking collectives, entering(): gathered = lax.all_gather(part, axis)  22 us
    ppermute x7, starting transfers between devices, exchange_in_pairs(): part = lax.ppermute(part, axis, [(d, d ^ mask) for d in range(ways)])  11.3 us
    all_to_all x1, waiting for transfers between devices, local(): lax.all_to_all(back_rows.reshape(peer_count, slot_count, flux_width), 'sp...  7.91 us
    ppermute x7, waiting for transfers between devices, exchange_in_pairs(): part = lax.ppermute(part, axis, [(d, d ^ mask) for d in range(ways)])  5.98 us
    ppermute x1, starting transfers between devices, extended(): lax.ppermute(tail, axis, [(i, (i + 1) % count) for i in range(ends)])  5.01 us
    all_to_all x1, starting transfers between devices, local(): lax.all_to_all(back_rows.reshape(peer_count, slot_count, flux_width), 'sp...  3.54 us
    all_to_all x1, starting transfers between devices, local(): lax.all_to_all(send_rows.reshape(peer_count, slot_count, flux_width), 'sp...  3.41 us
    slice x6, local copies, waits for them, and re-layouts, conv_taps(): columns.append(jnp.roll(lat_band, 1 - col_off, axis=1))  1.81 us
  transfers between devices with their start and end apart: 11, of which 4 were waited for; matrix products, arithmetic and copies ran while one was open for 9% of the time, Pallas kernels for 0%

profile of v1, /device:TPU:0, one launch (start us, length us, event | category | flops | bytes accessed | tf_op | source)
XLA Modules:
  0.0 76.2 jit_solution(11757250707547401241)
XLA Ops:
  0.7 5.0 %collective-permute-start = (bf16[1,256,256]{2,1,0:T(8,128)(2,1)}, bf16[1,256,256]{2,1,0:T(8,128)(2,1)S(1)}, u32[]{:S(2)}, u32[]{:S(2)}) collective-permute-start(bf16[1,256,256]{2,1,0:T(8,128)(2,1)} %bitcast.71), channel_id=1, source_target_pairs={{0,2},{2,4},{4,6},{6,8},{8,10},{10,12},{12,14},{1,3},{3,5},{5,7},{... | collective-permute-start | bytes 393224 | tf_op jit(solution)/shard_map/ppermute | solution.py:32
  5.7 1.3 %collective-permute-start.1 = (bf16[1,256,256]{2,1,0:T(8,128)(2,1)}, bf16[1,256,256]{2,1,0:T(8,128)(2,1)S(1)}, u32[]{:S(2)}, u32[]{:S(2)}) collective-permute-start(bf16[1,256,256]{2,1,0:T(8,128)(2,1)} %bitcast.72), channel_id=1, source_target_pairs={{2,0},{4,2},{6,4},{8,6},{10,8},{12,10},{14,12},{3,1},{5,3},{7,5},{... | collective-permute-start | bytes 393224 | tf_op jit(solution)/shard_map/ppermute | solution.py:34
  7.0 1.0 %fusion.47 = (bf16[1,255,256]{2,1,0:T(8,128)(2,1)S(1)}, bf16[1,255,256]{2,1,0:T(8,128)(2,1)S(1)}) fusion(bf16[1,256,256]{2,1,0:T(8,128)(2,1)} %bitcast.73), kind=kLoop, calls=%fused_computation.81 | loop fusion | bytes 522240 | tf_op jit(solution)/shard_map/jit(_roll_static)/slice | solution.py:58
  8.0 0.7 fusion.48
  8.7 0.8 %copy.35 = s32[1,256,2]{2,1,0:T(8,128)S(1)} copy(s32[1,256,2]{1,2,0:T(2,128)} %param.22) | data formatting | bytes 4096 | tf_op args[2]
  9.8 1.1 %reduce-window.6 = s32[8,4,128]{2,0,1:T(8,128)S(1)} reduce-window(s32[8,4,128]{2,0,1:T(8,128)S(1)} %fusion.41, s32[]{:T(128)} %constant.20.clone.1), window={size=1x1x128 pad=0_0x0_0x127_0}, to_apply=%region_4.5 | reduce-window | flops 520192 | bytes 32772 | tf_op jit(solution)/shard_map/reduce-window
  11.2 0.7 convert_element_type.74
  13.5 22.0 %all-gather.1 = f32[8,1,256]{2,1,0:T(1,128)S(1)} all-gather(f32[1,1,256]{2,1,0:T(1,128)S(1)} %bitcast.86), channel_id=2, replica_groups=mesh['groups'=2,'space'=8,'section'=2] {'space'}, dimensions={0}, use_global_device_ids=true | all-gather | bytes 9216 | tf_op jit(solution)/shard_map/all_gather | solution.py:43
  35.9 0.6 fusion.18
  37.1 1.6 %fusion.4 = bf16[1024,128]{1,0:T(8,128)(2,1)} fusion(s32[512]{0:T(512)S(1)} %multiply_add_fusion, f32[512,128]{1,0:T(8,128)S(1)} %bitcast.75, f32[512]{0:T(512)S(1)} %mul.149), kind=kOutput, calls=%fused_computation.7 | convolution fusion | flops 135004160 | bytes 528384 | tf_op jit(solution)/shard_map/dot_general | solution.py:76
  38.7 3.4 %all-to-all-start = ((bf16[8,128,128]{2,1,0:T(8,128)(2,1)}), bf16[8,128,128]{2,1,0:T(8,128)(2,1)S(1)}, u32[]{:S(2)}, u32[]{:S(2)}) async-start(bf16[8,128,128]{2,1,0:T(8,128)(2,1)} %bitcast.18), calls=%async_computation | async-start | bytes 524288 | tf_op jit(solution)/shard_map/all_to_all | solution.py:147
  42.8 1.9 %collective-permute-start.2 = (s32[1,128]{1,0:T(1,128)S(1)}, s32[1,128]{1,0:T(1,128)S(1)}, u32[]{:S(2)}, u32[]{:S(2)}) collective-permute-start(s32[1,128]{1,0:T(1,128)S(1)} %get-tuple-element.52), channel_id=1, source_target_pairs={{0,2},{2,0},{4,6},{6,4},{8,10},{10,8},{12,14},{14,12},{1,3},{3,1},... | collective-permute-start | bytes 1544 | tf_op jit(solution)/shard_map/ppermute | solution.py:19
  44.7 1.5 %collective-permute-start.3 = (s32[1,128]{1,0:T(1,128)S(1)}, s32[1,128]{1,0:T(1,128)S(1)}, u32[]{:S(2)}, u32[]{:S(2)}) collective-permute-start(s32[1,128]{1,0:T(1,128)S(1)} %get-tuple-element.51), channel_id=1, source_target_pairs={{0,4},{2,6},{4,0},{6,2},{8,12},{10,14},{12,8},{14,10},{1,5},{3,7},... | collective-permute-start | bytes 1544 | tf_op jit(solution)/shard_map/ppermute | solution.py:19
  46.3 2.8 %collective-permute-start.5 = (s32[1,128]{1,0:T(1,128)S(1)}, s32[1,128]{1,0:T(1,128)S(1)}, u32[]{:S(2)}, u32[]{:S(2)}) collective-permute-start(s32[1,128]{1,0:T(1,128)S(1)} %get-tuple-element.49), channel_id=1, source_target_pairs={{0,8},{2,10},{4,12},{6,14},{8,0},{10,2},{12,4},{14,6},{1,9},{3,11}... | collective-permute-start | bytes 1544 | tf_op jit(solution)/shard_map/ppermute | solution.py:19
  49.1 1.4 %collective-permute-start.6 = (s32[1,128]{1,0:T(1,128)S(1)}, s32[1,128]{1,0:T(1,128)S(1)}, u32[]{:S(2)}, u32[]{:S(2)}) collective-permute-start(s32[1,128]{1,0:T(1,128)S(1)} %get-tuple-element.48), channel_id=1, source_target_pairs={{0,10},{2,8},{4,14},{6,12},{8,2},{10,0},{12,6},{14,4},{1,11},{3,9}... | collective-permute-start | bytes 1544 | tf_op jit(solution)/shard_map/ppermute | solution.py:19
  50.6 3.4 %collective-permute-start.7 = (s32[1,128]{1,0:T(1,128)S(1)}, s32[1,128]{1,0:T(1,128)S(1)}, u32[]{:S(2)}, u32[]{:S(2)}) collective-permute-start(s32[1,128]{1,0:T(1,128)S(1)} %get-tuple-element.47), channel_id=1, source_target_pairs={{0,12},{2,14},{4,8},{6,10},{8,4},{10,6},{12,0},{14,2},{1,13},{3,15... | collective-permute-start | bytes 1544 | tf_op jit(solution)/shard_map/ppermute | solution.py:19
  54.5 1.5 %collective-permute-done.7 = s32[1,128]{1,0:T(1,128)S(1)} collective-permute-done((s32[1,128]{1,0:T(1,128)S(1)}, s32[1,128]{1,0:T(1,128)S(1)}, u32[]{:S(2)}, u32[]{:S(2)}) %collective-permute-start.7) | collective-permute-done | bytes 544 | tf_op jit(solution)/shard_map/ppermute | solution.py:19
  56.0 4.2 %collective-permute-done.8 = s32[1,128]{1,0:T(1,128)S(1)} collective-permute-done((s32[1,128]{1,0:T(1,128)S(1)}, s32[1,128]{1,0:T(1,128)S(1)}, u32[]{:S(2)}, u32[]{:S(2)}) %collective-permute-start.8) | collective-permute-done | bytes 544 | tf_op jit(solution)/shard_map/ppermute | solution.py:19
  60.3 0.8 %multiply_reduce_fusion.1 = (f32[256]{0:T(256)S(1)}, f32[256,192]{0,1:T(8,128)S(1)}) fusion(bf16[128,192]{0,1:T(8,128)(2,1)S(1)} %copy-done.12, bf16[1024,128]{1,0:T(8,128)(2,1)S(1)} %bitcast.76, s32[1024]{0:T(1024)S(1)} %bitcast.87, bf16[1,256,192]{1,2,0:T(8,128)(2,1)S(1)} %copy-done.11), kind=kOutput, calls=%fused_computation.37 | convolution fusion | flops 80183040 | bytes 611328 | tf_op jit(solution)/shard_map/dot_general | solution.py:162
  61.1 0.7 fusion.19
  61.9 1.2 %convolution_convert_fusion = bf16[1024,128]{1,0:T(8,128)(2,1)} fusion(bf16[256,192]{0,1:T(8,128)(2,1)S(1)} %fusion.19, bf16[192,128]{1,0:T(8,128)(2,1)S(1)} %copy-done.13, s32[1024]{0:T(1024)S(1)} %bitcast.88), kind=kOutput, calls=%fused_computation.8 | convolution fusion | flops 80117760 | bytes 413696 | tf_op jit(solution)/shard_map/dot_general | solution.py:175
  63.2 3.5 %all-to-all-start.1 = ((bf16[8,128,128]{2,1,0:T(8,128)(2,1)}), bf16[8,128,128]{2,1,0:T(8,128)(2,1)S(1)}, u32[]{:S(2)}, u32[]{:S(2)}) async-start(bf16[8,128,128]{2,1,0:T(8,128)(2,1)} %bitcast.20), calls=%async_computation.1 | async-start | bytes 524288 | tf_op jit(solution)/shard_map/all_to_all | solution.py:178
  67.0 7.9 %all-to-all-done.1 = bf16[8,128,128]{2,1,0:T(8,128)(2,1)S(1)} async-done(((bf16[8,128,128]{2,1,0:T(8,128)(2,1)}), bf16[8,128,128]{2,1,0:T(8,128)(2,1)S(1)}, u32[]{:S(2)}, u32[]{:S(2)}) %all-to-all-start.1) | async-done | bytes 262176 | tf_op jit(solution)/shard_map/all_to_all | solution.py:178
  75.4 0.8 %fusion.20 = bf16[1,1,256,256]{3,2,1,0:T(8,128)(2,1)} fusion(bf16[128,256]{1,0:T(8,128)(2,1)S(1)} %copy-done.4, bf16[256,256]{1,0:T(8,128)(2,1)S(1)} %fusion.18, f32[256]{0:T(256)S(1)} %bitcast.82, bf16[256,128]{1,0:T(8,128)(2,1)S(1)} %fusion.15), kind=kOutput, calls=%fused_computation.22 | convolution fusion | flops 17039360 | bytes 394240 | tf_op jit(solution)/shard_map/dot_general | solution.py:188
  (99 shorter events, 5.0 us)
Async XLA Ops:
  0.6 12.3 %copy-start = (bf16[9,256,256]{2,1,0:T(8,128)(2,1)S(1)}, bf16[9,256,256]{2,1,0:T(8,128)(2,1)}, u32[]{:S(2)}) copy-start(bf16[9,256,256]{2,1,0:T(8,128)(2,1)} %param.26) | copy-start | bytes 3538948
  0.6 11.5 %copy-start.6 = (f32[1,256,2]{1,2,0:T(2,128)S(1)}, f32[1,256,2]{1,2,0:T(2,128)}, u32[]{:S(2)}) copy-start(f32[1,256,2]{1,2,0:T(2,128)} %param.24) | copy-start | bytes 6148
  0.7 11.9 %collective-permute-start = (bf16[1,256,256]{2,1,0:T(8,128)(2,1)}, bf16[1,256,256]{2,1,0:T(8,128)(2,1)S(1)}, u32[]{:S(2)}, u32[]{:S(2)}) collective-permute-start(bf16[1,256,256]{2,1,0:T(8,128)(2,1)} %bitcast.71), channel_id=1, source_target_pairs={{0,2},{2,4},{4,6},{6,8},{8,10},{10,12},{12,14},{1,3},{3,5},{5,7},{... | collective-permute-start | bytes 393224 | tf_op jit(solution)/shard_map/ppermute | solution.py:32
  5.7 7.2 %collective-permute-start.1 = (bf16[1,256,256]{2,1,0:T(8,128)(2,1)}, bf16[1,256,256]{2,1,0:T(8,128)(2,1)S(1)}, u32[]{:S(2)}, u32[]{:S(2)}) collective-permute-start(bf16[1,256,256]{2,1,0:T(8,128)(2,1)} %bitcast.72), channel_id=1, source_target_pairs={{2,0},{4,2},{6,4},{8,6},{10,8},{12,10},{14,12},{3,1},{5,3},{7,5},{... | collective-permute-start | bytes 393224 | tf_op jit(solution)/shard_map/ppermute | solution.py:34
  13.0 22.5 %copy-start.2 = (bf16[256,256]{1,0:T(8,128)(2,1)S(1)}, bf16[256,256]{1,0:T(8,128)(2,1)}, u32[]{:S(2)}) copy-start(bf16[256,256]{1,0:T(8,128)(2,1)} %param.27) | copy-start | bytes 393220
  13.0 22.9 %copy-start.7 = (bf16[1024,256]{1,0:T(8,128)(2,1)S(1)}, bf16[1024,256]{1,0:T(8,128)(2,1)}, u32[]{:S(2)}) copy-start(bf16[1024,256]{1,0:T(8,128)(2,1)} %param.30) | copy-start | bytes 1572868
  13.0 22.9 %copy-start.8 = (bf16[256,1024]{1,0:T(8,128)(2,1)S(1)}, bf16[256,1024]{1,0:T(8,128)(2,1)}, u32[]{:S(2)}) copy-start(bf16[256,1024]{1,0:T(8,128)(2,1)} %param.29) | copy-start | bytes 1572868
  13.0 22.9 %copy-start.14 = (f32[256]{0:T(256)S(1)}, f32[256]{0:T(256)}, u32[]{:S(2)}) copy-start(f32[256]{0:T(256)} %param.28) | copy-start | bytes 3076
  36.9 23.4 %copy-start.11 = (bf16[1,256,192]{1,2,0:T(8,128)(2,1)S(1)}, bf16[1,256,192]{1,2,0:T(8,128)(2,1)}, u32[]{:S(2)}) copy-start(bf16[1,256,192]{1,2,0:T(8,128)(2,1)} %param.21) | copy-start | bytes 294916
  36.9 23.3 %copy-start.12 = (bf16[128,192]{0,1:T(8,128)(2,1)S(1)}, bf16[128,192]{0,1:T(8,128)(2,1)}, u32[]{:S(2)}) copy-start(bf16[128,192]{0,1:T(8,128)(2,1)} %param.32) | copy-start | bytes 147460
  37.0 24.1 %copy-start.9 = (bf16[768,192]{0,1:T(8,128)(2,1)S(1)}, bf16[768,192]{0,1:T(8,128)(2,1)}, u32[]{:S(2)}) copy-start(bf16[768,192]{0,1:T(8,128)(2,1)} %param.35) | copy-start | bytes 884740
  37.0 24.1 %copy-start.10 = (bf16[192,768]{1,0:T(8,128)(2,1)S(1)}, bf16[192,768]{1,0:T(8,128)(2,1)}, u32[]{:S(2)}) copy-start(bf16[192,768]{1,0:T(8,128)(2,1)} %param.34) | copy-start | bytes 884740
  37.0 24.1 %copy-start.15 = (f32[192]{0:T(256)S(1)}, f32[192]{0:T(256)}, u32[]{:S(2)}) copy-start(f32[192]{0:T(256)} %param.33) | copy-start | bytes 2308
  38.7 21.6 %all-to-all-start = ((bf16[8,128,128]{2,1,0:T(8,128)(2,1)}), bf16[8,128,128]{2,1,0:T(8,128)(2,1)S(1)}, u32[]{:S(2)}, u32[]{:S(2)}) async-start(bf16[8,128,128]{2,1,0:T(8,128)(2,1)} %bitcast.18), calls=%async_computation | async-start | bytes 524288 | tf_op jit(solution)/shard_map/all_to_all | solution.py:147
  42.8 7.8 %collective-permute-start.2 = (s32[1,128]{1,0:T(1,128)S(1)}, s32[1,128]{1,0:T(1,128)S(1)}, u32[]{:S(2)}, u32[]{:S(2)}) collective-permute-start(s32[1,128]{1,0:T(1,128)S(1)} %get-tuple-element.52), channel_id=1, source_target_pairs={{0,2},{2,0},{4,6},{6,4},{8,10},{10,8},{12,14},{14,12},{1,3},{3,1},... | collective-permute-start | bytes 1544 | tf_op jit(solution)/shard_map/ppermute | solution.py:19
  44.7 9.3 %collective-permute-start.3 = (s32[1,128]{1,0:T(1,128)S(1)}, s32[1,128]{1,0:T(1,128)S(1)}, u32[]{:S(2)}, u32[]{:S(2)}) collective-permute-start(s32[1,128]{1,0:T(1,128)S(1)} %get-tuple-element.51), channel_id=1, source_target_pairs={{0,4},{2,6},{4,0},{6,2},{8,12},{10,14},{12,8},{14,10},{1,5},{3,7},... | collective-permute-start | bytes 1544 | tf_op jit(solution)/shard_map/ppermute | solution.py:19
  46.2 7.9 %collective-permute-start.4 = (s32[1,128]{1,0:T(1,128)S(1)}, s32[1,128]{1,0:T(1,128)S(1)}, u32[]{:S(2)}, u32[]{:S(2)}) collective-permute-start(s32[1,128]{1,0:T(1,128)S(1)} %get-tuple-element.50), channel_id=1, source_target_pairs={{0,6},{2,4},{4,2},{6,0},{8,14},{10,12},{12,10},{14,8},{1,7},{3,5},... | collective-permute-start | bytes 1544 | tf_op jit(solution)/shard_map/ppermute | solution.py:19
  46.3 7.8 %collective-permute-start.5 = (s32[1,128]{1,0:T(1,128)S(1)}, s32[1,128]{1,0:T(1,128)S(1)}, u32[]{:S(2)}, u32[]{:S(2)}) collective-permute-start(s32[1,128]{1,0:T(1,128)S(1)} %get-tuple-element.49), channel_id=1, source_target_pairs={{0,8},{2,10},{4,12},{6,14},{8,0},{10,2},{12,4},{14,6},{1,9},{3,11}... | collective-permute-start | bytes 1544 | tf_op jit(solution)/shard_map/ppermute | solution.py:19
  49.1 5.4 %collective-permute-start.6 = (s32[1,128]{1,0:T(1,128)S(1)}, s32[1,128]{1,0:T(1,128)S(1)}, u32[]{:S(2)}, u32[]{:S(2)}) collective-permute-start(s32[1,128]{1,0:T(1,128)S(1)} %get-tuple-element.48), channel_id=1, source_target_pairs={{0,10},{2,8},{4,14},{6,12},{8,2},{10,0},{12,6},{14,4},{1,11},{3,9}... | collective-permute-start | bytes 1544 | tf_op jit(solution)/shard_map/ppermute | solution.py:19
  50.6 5.4 %collective-permute-start.7 = (s32[1,128]{1,0:T(1,128)S(1)}, s32[1,128]{1,0:T(1,128)S(1)}, u32[]{:S(2)}, u32[]{:S(2)}) collective-permute-start(s32[1,128]{1,0:T(1,128)S(1)} %get-tuple-element.47), channel_id=1, source_target_pairs={{0,12},{2,14},{4,8},{6,10},{8,4},{10,6},{12,0},{14,2},{1,13},{3,15... | collective-permute-start | bytes 1544 | tf_op jit(solution)/shard_map/ppermute | solution.py:19
  54.0 6.3 %collective-permute-start.8 = (s32[1,128]{1,0:T(1,128)S(1)}, s32[1,128]{1,0:T(1,128)S(1)}, u32[]{:S(2)}, u32[]{:S(2)}) collective-permute-start(s32[1,128]{1,0:T(1,128)S(1)} %get-tuple-element.46), channel_id=1, source_target_pairs={{0,14},{2,12},{4,10},{6,8},{8,6},{10,4},{12,2},{14,0},{1,15},{3,13... | collective-permute-start | bytes 1544 | tf_op jit(solution)/shard_map/ppermute | solution.py:19
  61.9 13.5 %copy-start.16 = (bf16[256,192]{0,1:T(8,128)(2,1)}, bf16[256,192]{0,1:T(8,128)(2,1)S(1)}, u32[]{:S(2)}) copy-start(bf16[256,192]{0,1:T(8,128)(2,1)S(1)} %fusion.19) | copy-start | bytes 294916
  63.2 12.2 %copy-start.4 = (bf16[128,256]{1,0:T(8,128)(2,1)S(1)}, bf16[128,256]{1,0:T(8,128)(2,1)}, u32[]{:S(2)}) copy-start(bf16[128,256]{1,0:T(8,128)(2,1)} %param.37) | copy-start | bytes 196612
  63.2 11.7 %all-to-all-start.1 = ((bf16[8,128,128]{2,1,0:T(8,128)(2,1)}), bf16[8,128,128]{2,1,0:T(8,128)(2,1)S(1)}, u32[]{:S(2)}, u32[]{:S(2)}) async-start(bf16[8,128,128]{2,1,0:T(8,128)(2,1)} %bitcast.20), calls=%async_computation.1 | async-start | bytes 524288 | tf_op jit(solution)/shard_map/all_to_all | solution.py:178
  (4 other events, 10.1 us)
